TPU v7x, 32 devices: a whole 2x2x4 slice. The times are simulated.
32 devices in a mesh: row: 8 (over y, x, core), col: 4 (over z).
Axes of the slice: x: 2, y: 2, z: 4, core: 2. Of those that a mesh axis runs over, the one named last changes fastest.
Arguments:
- matrix: float32 [10240, 10240], P('row', 'col'), may hold values from 0 to 1.5, as said below
Outputs:
- factored: float32 [10240, 10240], P('row', 'col')
Inputs may be any that keep to these rules, and one draw needn't show every extreme that they name: A Gaussian kernel matrix over random embeddings plus a ridge on the diagonal, stored block-cyclically; symmetric positive definite, diagonal entries near 1.5.
All inputs are finite; a program needn't handle non-finite values.
Results may differ from a plain program's by a relative error of at most 0.0003.
Values sent between devices are 32-bit elements; how exact they have to be, the bound alone decides.
A program may use at most 192 MiB of HBM per device.

v0:
```python
import jax
import jax.numpy as jnp
from jax import lax
from jax.sharding import PartitionSpec as P

NB = 256


def spread(array, axis, root):
    mine = lax.axis_index(axis) == root
    return lax.psum(jnp.where(mine, array, jnp.zeros_like(array)), axis)


def make_panel(col_block, k, row_tiles):
    tiles_here = col_block.shape[0] // NB
    diag_block = spread(col_block[:NB], "row", k)
    factor_low = jnp.linalg.cholesky(diag_block)
    inverse = lax.linalg.triangular_solve(
        factor_low, jnp.eye(NB, dtype=factor_low.dtype), left_side=True, lower=True
    )
    scaled = jnp.dot(col_block, inverse.T, precision=lax.Precision.HIGHEST)
    tile_copy = jnp.tile(factor_low, (tiles_here, 1))
    marks = row_tiles[:, None]
    row_panel = jnp.where(marks > k, scaled, jnp.where(marks == k, tile_copy, 0.0))
    return spread(row_panel, "col", k)


def column_panel(row_panel):
    tiles_here = row_panel.shape[0] // NB
    n_row = lax.axis_size("row")
    n_col = lax.axis_size("col")
    groups = n_row // n_col
    pieces = [spread(row_panel, "row", lax.axis_index("col") + m * n_col) for m in range(groups)]
    chosen = jnp.stack(pieces).reshape(groups, tiles_here, NB, NB)
    return chosen.transpose(1, 0, 2, 3).reshape(tiles_here * groups * NB, NB)


def local(matrix):
    local_rows, local_cols = matrix.shape
    n_row = lax.axis_size("row")
    n_col = lax.axis_size("col")
    row_index = lax.axis_index("row")
    col_index = lax.axis_index("col")
    row_tiles = jnp.arange(local_rows, dtype=jnp.int32) // NB * n_row + row_index
    col_tiles = jnp.arange(local_cols, dtype=jnp.int32) // NB * n_col + col_index
    highest = lax.Precision.HIGHEST
    panel_first = make_panel(matrix[:, :NB], 0, row_tiles)
    across_first = column_panel(panel_first)
    rows_first = panel_first * (row_tiles > 0)[:, None]
    cols_first = across_first * (col_tiles > 0)[:, None]
    current = matrix - jnp.dot(rows_first, cols_first.T, precision=highest)
    panel_second = make_panel(current[:, :NB], 1, row_tiles)
    across_second = column_panel(panel_second)
    rows_second = panel_second * (row_tiles > 1)[:, None]
    cols_second = across_second * (col_tiles > 1)[:, None]
    current = current - jnp.dot(rows_second, cols_second.T, precision=highest)
    lead_cols = current[:, :NB]
    lead_cols = jnp.where(col_index == 0, panel_first, lead_cols)
    lead_cols = jnp.where(col_index == 1, panel_second, lead_cols)
    current = current.at[:, :NB].set(lead_cols)
    zero_mask = (row_tiles[:, None] == 0) & (col_tiles[None, :] > 0) | (row_tiles[:, None] == 1) & (
        col_tiles[None, :] > 1
    )
    return jnp.where(zero_mask, 0.0, current)


def solution(mesh):
    placed = (P("row", "col"),)
    return jax.shard_map(
        local, mesh=mesh, in_specs=placed, out_specs=P("row", "col"), check_vma=False
    )
```

profile of v0, /device:TPU:0, one launch (start us, length us, event | category | flops | bytes accessed | tf_op | source)
XLA Modules:
  0.0 600.5 jit_solution(3242503386733762147)
XLA Ops:
  6.5 13.9 %copy.18 = f32[1280,2560]{0,1:T(8,128)} copy(f32[1280,2560]{1,0:T(8,128)} %param.6) | data formatting | bytes 26214400 | tf_op args[0]
  20.4 1.7 slice_select_fusion.1
  22.2 56.6 %all-reduce.10.cloned.1.call-done = f32[256,256]{0,1:T(8,128)} async-done(((f32[256,256]{0,1:T(8,128)}), f32[256,256]{0,1:T(8,128)}) %all-reduce.10.cloned.1.call-update) | async-done | bytes 262160 | tf_op jit(solution)/shard_map/psum | solution.py:11
  78.8 1.1 copy.13
  79.9 1.0 fusion.16
  80.9 11.7 %cholesky.130 = f32[128,128]{1,0:T(8,128)S(1)} custom-call(f32[128,128]{1,0:T(8,128)S(1)} %cholesky.194), custom_call_target="Cholesky" | custom-call | tf_op jit(solution)/shard_map/jit(cholesky)/cholesky | solution.py:17
  92.7 9.8 %custom-call.13 = f32[1,128,128]{1,2,0:T(8,128)S(1)} custom-call(f32[1,128,128]{2,1,0:T(8,128)S(1)} %get-tuple-element.74), custom_call_target="InvertDiagBlocksLowerTriangular" | custom-call | tf_op jit(solution)/shard_map/jit(cholesky)/cholesky | solution.py:17
  103.0 11.7 %cholesky.147 = f32[128,128]{1,0:T(8,128)S(1)} custom-call(f32[128,128]{1,0:T(8,128)S(1)} %convolution_subtract_fusion.5), custom_call_target="Cholesky" | custom-call | tf_op jit(solution)/shard_map/jit(cholesky)/cholesky | solution.py:17
  114.8 0.7 compare_reduce_fusion.2
  116.9 4.6 while.5
  118.1 1.3 bitcast_dynamic-update-slice_fusion.4
  120.1 1.3 bitcast_dynamic-update-slice_fusion.4
  121.5 19.7 %custom-call.14 = f32[2,128,128]{1,2,0:T(8,128)S(1)} custom-call(f32[2,128,128]{2,1,0:T(8,128)S(1)} %get-tuple-element.33), custom_call_target="InvertDiagBlocksLowerTriangular" | custom-call | tf_op jit(solution)/shard_map/triangular_solve/custom-call.0 | solution.py:18
  142.6 3.7 fusion.2
  146.3 59.6 %all-reduce.12.cloned.1.call-done = f32[1280,256]{0,1:T(8,128)} async-done(((f32[1280,256]{0,1:T(8,128)}), f32[1280,256]{0,1:T(8,128)}) %all-reduce.12.cloned.1.call-update) | async-done | bytes 1310736 | tf_op jit(solution)/shard_map/psum | solution.py:11
  205.9 1.5 broadcast_select_fusion.2
  207.4 1.5 copy.15
  208.9 1.5 copy.16
  210.5 64.3 %all-reduce.20.cloned.1.call-done = (f32[1,5,256,256]{3,2,1,0:T(8,128)}, f32[1,5,256,256]{3,2,1,0:T(8,128)}) async-done(((f32[1,5,256,256]{3,2,1,0:T(8,128)}, f32[1,5,256,256]{3,2,1,0:T(8,128)}), (f32[1,5,256,256]{3,2,1,0:T(8,128)}, f32[1,5,256,256]{3,2,1,0:T(8,128)})) %all-reduce.20.cloned.1.call-update) | async-done | bytes 2621456 | tf_op jit(solution)/shard_map/psum | solution.py:11
  274.8 2.0 maximum_bitcast_fusion
  277.5 0.9 copy-done.1
  278.4 15.0 %convolution_subtract_fusion.1 = f32[1280,2560]{0,1:T(8,128)S(1)} fusion(f32[1280,2560]{0,1:T(8,128)} %copy.18, f32[2560,256]{1,0:T(8,128)S(1)} %bitcast_multiply_fusion.1, f32[1280,256]{0,1:T(8,128)S(1)} %copy-done.1, f32[1280]{0:T(1024)S(1)} %fusion.53), kind=kOutput, calls=%fused_computation.5 | convolution fusion | flops 10069934080 | bytes 30151680 | tf_op jit(solution)/shard_map/dot_general | solution.py:51
  293.4 4.9 copy-done
  299.3 53.3 %all-reduce.14.cloned.1.call-done = f32[256,256]{0,1:T(8,128)} async-done(((f32[256,256]{0,1:T(8,128)}), f32[256,256]{0,1:T(8,128)}) %all-reduce.14.cloned.1.call-update) | async-done | bytes 262160 | tf_op jit(solution)/shard_map/psum | solution.py:11
  352.7 1.1 copy.20
  353.7 1.0 fusion.15
  354.7 11.7 %cholesky.164 = f32[128,128]{1,0:T(8,128)S(1)} custom-call(f32[128,128]{1,0:T(8,128)S(1)} %cholesky.197), custom_call_target="Cholesky" | custom-call | tf_op jit(solution)/shard_map/jit(cholesky)/cholesky | solution.py:17
  366.5 9.8 %custom-call.15 = f32[1,128,128]{1,2,0:T(8,128)S(1)} custom-call(f32[1,128,128]{2,1,0:T(8,128)S(1)} %get-tuple-element.70), custom_call_target="InvertDiagBlocksLowerTriangular" | custom-call | tf_op jit(solution)/shard_map/jit(cholesky)/cholesky | solution.py:17
  376.8 11.7 %cholesky.181 = f32[128,128]{1,0:T(8,128)S(1)} custom-call(f32[128,128]{1,0:T(8,128)S(1)} %convolution_subtract_fusion.4), custom_call_target="Cholesky" | custom-call | tf_op jit(solution)/shard_map/jit(cholesky)/cholesky | solution.py:17
  391.2 4.3 while.6
  392.1 1.3 bitcast_dynamic-update-slice_fusion.5
  394.2 1.3 bitcast_dynamic-update-slice_fusion.5
  395.5 19.7 %custom-call.16 = f32[2,128,128]{1,2,0:T(8,128)S(1)} custom-call(f32[2,128,128]{2,1,0:T(8,128)S(1)} %get-tuple-element.34), custom_call_target="InvertDiagBlocksLowerTriangular" | custom-call | tf_op jit(solution)/shard_map/triangular_solve/custom-call.0 | solution.py:18
  416.1 1.2 tile.20
  417.3 1.7 copy.21
  419.0 3.7 fusion
  422.8 59.6 %all-reduce.16.cloned.1.call-done = f32[1280,256]{0,1:T(8,128)} async-done(((f32[1280,256]{0,1:T(8,128)}), f32[1280,256]{0,1:T(8,128)}) %all-reduce.16.cloned.1.call-update) | async-done | bytes 1310736 | tf_op jit(solution)/shard_map/psum | solution.py:11
  482.4 2.6 broadcast_select_fusion.3
  485.0 2.8 copy.23
  487.8 1.5 copy.24
  489.3 0.9 compare_reduce_fusion.4
  490.3 63.5 %all-reduce.18.cloned.1.call-done = (f32[1,5,256,256]{3,2,1,0:T(8,128)}, f32[1,5,256,256]{3,2,1,0:T(8,128)}) async-done(((f32[1,5,256,256]{3,2,1,0:T(8,128)}, f32[1,5,256,256]{3,2,1,0:T(8,128)}), (f32[1,5,256,256]{3,2,1,0:T(8,128)}, f32[1,5,256,256]{3,2,1,0:T(8,128)})) %all-reduce.18.cloned.1.call-update) | async-done | bytes 2621456 | tf_op jit(solution)/shard_map/psum | solution.py:11
  553.7 2.0 maximum_bitcast_fusion.1
  556.4 0.9 copy-done.2
  557.3 15.0 %convolution_subtract_fusion = f32[1280,2560]{0,1:T(8,128)S(1)} fusion(f32[1280,2560]{0,1:T(8,128)} %copy-done, f32[2560,256]{1,0:T(8,128)S(1)} %bitcast_multiply_fusion, f32[1280,256]{0,1:T(8,128)S(1)} %copy-done.2, f32[1280]{0:T(1024)S(1)} %fusion.54), kind=kOutput, calls=%fused_computation.4 | convolution fusion | flops 10069934080 | bytes 30151680 | tf_op jit(solution)/shard_map/dot_general | solution.py:56
  572.3 1.3 select_dynamic-update-slice_fusion
  573.6 5.9 or_select_fusion
  579.5 13.9 %copy.27 = f32[1280,2560]{1,0:T(8,128)} copy(f32[1280,2560]{0,1:T(8,128)} %or_select_fusion) | data formatting | bytes 26214400 | tf_op jit(solution)/shard_map/jit(_where)/select_n | solution.py:64
  (64 shorter events, 10.1 us)
Async XLA Ops:
  6.5 72.3 %all-reduce.10.cloned.1.call-start = ((), (), s32[]{:S(2)}) async-start(), calls=%async_computation | async-start | bytes 524288 | tf_op jit(solution)/shard_map/psum | solution.py:11
  22.1 183.8 %all-reduce.12.cloned.1.call-start = ((), (), s32[]{:S(2)}) async-start(), calls=%async_computation.1 | async-start | bytes 2621440 | tf_op jit(solution)/shard_map/psum | solution.py:11
  146.3 128.6 %all-reduce.20.cloned.1.call-start = ((), (), s32[]{:S(2)}) async-start(), calls=%async_computation.5 | async-start | bytes 5242880 | tf_op jit(solution)/shard_map/psum | solution.py:11
  210.4 142.2 %all-reduce.14.cloned.1.call-start = ((), (), s32[]{:S(2)}) async-start(), calls=%async_computation.2 | async-start | bytes 524288 | tf_op jit(solution)/shard_map/psum | solution.py:11
  277.0 1.3 copy-start.1
  293.4 5.0 copy-start
  299.1 183.3 %all-reduce.16.cloned.1.call-start = ((), (), s32[]{:S(2)}) async-start(), calls=%async_computation.3 | async-start | bytes 2621440 | tf_op jit(solution)/shard_map/psum | solution.py:11
  422.8 131.0 %all-reduce.18.cloned.1.call-start = ((), (), s32[]{:S(2)}) async-start(), calls=%async_computation.4 | async-start | bytes 5242880 | tf_op jit(solution)/shard_map/psum | solution.py:11
  555.9 1.3 copy-start.2
Sparse Core Ops, SparseCore 0:
  22.2 56.5 all-reduce.9
  146.4 59.4 all-reduce.11
  210.6 64.2 all-reduce.19
  299.2 53.4 all-reduce.13
  422.9 59.4 all-reduce.15
  489.4 64.2 all-reduce.17
where the time goes:
time: 610 us; the launch traced here: 601 us
  waiting for transfers between devices  357 us (59%)
  other arithmetic  130 us (21%)
  local copies, waits for them, and re-layouts  55.9 us (9%)
  matrix products  40.2 us (7%)
  between operations  16.7 us (3%)
    psum x6, waiting for transfers between devices, spread(): return lax.psum(jnp.where(mine, array, jnp.zeros_like(array)), axis)  357 us
    another operation x13, other arithmetic, make_panel(): factor_low = jnp.linalg.cholesky(diag_block)  68.7 us
    another operation x5, other arithmetic, make_panel(): lax.linalg.triangular_solve(factor_low, jnp.eye(NB, dtype=factor_low.dtyp...  39.4 us
    unnamed x7, local copies, waits for them, and re-layouts  20.6 us
    dot_general x1, matrix products, local(): current = matrix - jnp.dot(rows_first, cols_first.T, precision=highest)  15 us
    dot_general x1, matrix products, local(): current = current - jnp.dot(rows_second, cols_second.T, precision=highest)  15 us
    select_n x1, local copies, waits for them, and re-layouts, local(): return jnp.where(zero_mask, 0.0, current)  13.9 us
  transfers between devices with their start and end apart: 6, of which 6 were waited for; matrix products, arithmetic and copies ran while one was open for 0% of the time, Pallas kernels for 0%

commit v1 on v0

--- a/solution.py
+++ b/solution.py
@@ -8,7 +8,7 @@
 
 def spread(array, axis, root):
     mine = lax.axis_index(axis) == root
-    return lax.psum(jnp.where(mine, array, jnp.zeros_like(array)), axis)
+    return jnp.sum(lax.all_gather(jnp.where(mine, array, jnp.zeros_like(array)), axis), axis=0)
 
 
 def make_panel(col_block, k, row_tiles):

time: 610 us -> 809 us (1.33)
  waiting for transfers between devices: 357 us -> 478 us
  local copies, waits for them, and re-layouts: 55.9 us -> 110 us
  other arithmetic: 130 us -> 153 us
    all_gather x0 -> x8, waiting for transfers between devices: none -> 476 us  [spread(): lax.all_gather(jnp.where(mine, array, jnp.zeros_like(array)), axis)]
    psum x6 -> x0, waiting for transfers between devices: 357 us -> none  [spread(): return lax.psum(jnp.where(mine, array, jnp.zeros_like(array)), axis)]
    unnamed x7 -> x17, local copies, waits for them, and re-layouts: 20.6 us -> 58.5 us
    reduce_sum x0 -> x8, other arithmetic: none -> 26.5 us  [spread(): jnp.sum(lax.all_gather(jnp.where(mine, array, jnp.zeros_like(array)), axi...]
    all_gather x0 -> x2, local copies, waits for them, and re-layouts: none -> 14.4 us  [spread(): lax.all_gather(jnp.where(mine, array, jnp.zeros_like(array)), axis)]
    reduce_sum x0 -> x6, local copies, waits for them, and re-layouts: none -> 11.7 us  [spread(): jnp.sum(lax.all_gather(jnp.where(mine, array, jnp.zeros_like(array)), axi...]
  transfers between devices with their start and end apart: 6 -> 8, of which waited for: 6 -> 8; matrix products, arithmetic and copies ran while one was open for 0% -> 4% of each run, Pallas kernels for 0% -> 0%
where the time goes in v1:
time: 809 us; the launch traced here: 799 us
  waiting for transfers between devices  478 us (59%)
  other arithmetic  153 us (19%)
  local copies, waits for them, and re-layouts  110 us (14%)
  matrix products  40.2 us (5%)
  between operations  16.6 us (2%)
    all_gather x8, waiting for transfers between devices, spread(): lax.all_gather(jnp.where(mine, array, jnp.zeros_like(array)), axis)  476 us
    another operation x13, other arithmetic, make_panel(): factor_low = jnp.linalg.cholesky(diag_block)  68.7 us
    unnamed x17, local copies, waits for them, and re-layouts  58.5 us
    another operation x5, other arithmetic, make_panel(): lax.linalg.triangular_solve(factor_low, jnp.eye(NB, dtype=factor_low.dtyp...  39.4 us
    reduce_sum x8, other arithmetic, spread(): jnp.sum(lax.all_gather(jnp.where(mine, array, jnp.zeros_like(array)), axi...  26.5 us
  transfers between devices with their start and end apart: 8, of which 8 were waited for; matrix products, arithmetic and copies ran while one was open for 4% of the time, Pallas kernels for 0%

profile of v1, /device:TPU:0, one launch (start us, length us, event | category | flops | bytes accessed | tf_op | source)
XLA Modules:
  0.0 798.7 jit_solution(5499515363278939882)
XLA Ops:
  6.5 13.9 %copy.42 = f32[1280,2560]{0,1:T(8,128)} copy(f32[1280,2560]{1,0:T(8,128)} %param.6) | data formatting | bytes 26214400 | tf_op args[0]
  20.4 1.7 slice_select_fusion.1
  22.3 30.9 %all-gather.17.cloned.1.call-done = f32[2048,256]{0,1:T(8,128)} async-done(((f32[256,256]{0,1:T(8,128)}), f32[2048,256]{0,1:T(8,128)}) %all-gather.17.cloned.1.call-update) | async-done | bytes 2097168 | tf_op jit(solution)/shard_map/all_gather | solution.py:11
  53.1 2.5 copy.55
  56.3 11.7 %cholesky.130 = f32[128,128]{1,0:T(8,128)S(1)} custom-call(f32[128,128]{1,0:T(8,128)S(1)} %cholesky.194), custom_call_target="Cholesky" | custom-call | tf_op jit(solution)/shard_map/jit(cholesky)/cholesky | solution.py:17
  68.1 9.8 %custom-call.13 = f32[1,128,128]{1,2,0:T(8,128)S(1)} custom-call(f32[1,128,128]{2,1,0:T(8,128)S(1)} %get-tuple-element.70), custom_call_target="InvertDiagBlocksLowerTriangular" | custom-call | tf_op jit(solution)/shard_map/jit(cholesky)/cholesky | solution.py:17
  78.4 11.7 %cholesky.147 = f32[128,128]{1,0:T(8,128)S(1)} custom-call(f32[128,128]{1,0:T(8,128)S(1)} %convolution_subtract_fusion.5), custom_call_target="Cholesky" | custom-call | tf_op jit(solution)/shard_map/jit(cholesky)/cholesky | solution.py:17
  92.3 4.2 while.5
  96.5 19.7 %custom-call.14 = f32[2,128,128]{1,2,0:T(8,128)S(1)} custom-call(f32[2,128,128]{2,1,0:T(8,128)S(1)} %get-tuple-element.33), custom_call_target="InvertDiagBlocksLowerTriangular" | custom-call | tf_op jit(solution)/shard_map/triangular_solve/custom-call.0 | solution.py:18
  117.6 3.7 fusion.2
  121.4 98.1 %all-gather.19.cloned.1.call-done = f32[5120,256]{0,1:T(8,128)} async-done(((f32[1280,256]{0,1:T(8,128)}), f32[5120,256]{0,1:T(8,128)}) %all-gather.19.cloned.1.call-update) | async-done | bytes 5242896 | tf_op jit(solution)/shard_map/all_gather | solution.py:11
  219.6 7.2 reshape.215
  226.8 5.6 reduce_sum.73
  232.4 1.7 broadcast_select_fusion.2
  234.9 60.7 %all-gather.21.cloned.1.call-done = f32[10240,256]{0,1:T(8,128)} async-done(((f32[1280,256]{0,1:T(8,128)}), f32[10240,256]{0,1:T(8,128)}) %all-gather.21.cloned.1.call-update) | async-done | bytes 10485776 | tf_op jit(solution)/shard_map/all_gather | solution.py:11
  295.7 8.3 %copy.56 = f32[32,8,8,1280]{3,2,1,0:T(8,128)S(1)} copy(f32[32,8,8,1280]{3,1,2,0:T(8,128)} %bitcast.120) | data formatting | bytes 20971520
  304.0 3.6 bitcast_reduce_fusion.3
  307.5 2.8 copy.39
  310.3 50.3 %all-gather.23.cloned.1.call-done = f32[10240,256]{0,1:T(8,128)} async-done(((f32[1280,256]{0,1:T(8,128)}), f32[10240,256]{0,1:T(8,128)}) %all-gather.23.cloned.1.call-update) | async-done | bytes 10485776 | tf_op jit(solution)/shard_map/all_gather | solution.py:11
  360.6 8.7 %copy.57 = f32[32,8,8,1280]{3,2,1,0:T(8,128)S(1)} copy(f32[32,8,8,1280]{3,1,2,0:T(8,128)} %bitcast.121) | data formatting | bytes 20971520
  369.3 3.5 bitcast_reduce_fusion.2
  372.8 2.9 copy.40
  377.9 15.0 %convolution_subtract_fusion.1 = f32[1280,2560]{0,1:T(8,128)S(1)} fusion(f32[1280,2560]{0,1:T(8,128)} %copy.42, f32[2560,256]{1,0:T(8,128)S(1)} %bitcast_multiply_fusion.1, f32[1280,256]{0,1:T(8,128)S(1)} %reduce_sum.73, f32[1280]{0:T(1024)S(1)} %fusion.53), kind=kOutput, calls=%fused_computation.5 | convolution fusion | flops 10069934080 | bytes 30151680 | tf_op jit(solution)/shard_map/dot_general | solution.py:51
  392.9 4.9 copy-done
  398.9 28.0 %all-gather.25.cloned.1.call-done = f32[2048,256]{0,1:T(8,128)} async-done(((f32[256,256]{0,1:T(8,128)}), f32[2048,256]{0,1:T(8,128)}) %all-gather.25.cloned.1.call-update) | async-done | bytes 2097168 | tf_op jit(solution)/shard_map/all_gather | solution.py:11
  426.9 2.5 copy.58
  430.1 11.7 %cholesky.164 = f32[128,128]{1,0:T(8,128)S(1)} custom-call(f32[128,128]{1,0:T(8,128)S(1)} %cholesky.197), custom_call_target="Cholesky" | custom-call | tf_op jit(solution)/shard_map/jit(cholesky)/cholesky | solution.py:17
  441.9 9.8 %custom-call.15 = f32[1,128,128]{1,2,0:T(8,128)S(1)} custom-call(f32[1,128,128]{2,1,0:T(8,128)S(1)} %get-tuple-element.66), custom_call_target="InvertDiagBlocksLowerTriangular" | custom-call | tf_op jit(solution)/shard_map/jit(cholesky)/cholesky | solution.py:17
  452.2 11.7 %cholesky.181 = f32[128,128]{1,0:T(8,128)S(1)} custom-call(f32[128,128]{1,0:T(8,128)S(1)} %convolution_subtract_fusion.4), custom_call_target="Cholesky" | custom-call | tf_op jit(solution)/shard_map/jit(cholesky)/cholesky | solution.py:17
  466.6 4.3 while.6
  470.9 19.7 %custom-call.16 = f32[2,128,128]{1,2,0:T(8,128)S(1)} custom-call(f32[2,128,128]{2,1,0:T(8,128)S(1)} %get-tuple-element.34), custom_call_target="InvertDiagBlocksLowerTriangular" | custom-call | tf_op jit(solution)/shard_map/triangular_solve/custom-call.0 | solution.py:18
  492.6 1.7 copy.45
  494.3 3.8 fusion
  498.2 98.1 %all-gather.27.cloned.1.call-done = f32[5120,256]{0,1:T(8,128)} async-done(((f32[1280,256]{0,1:T(8,128)}), f32[5120,256]{0,1:T(8,128)}) %all-gather.27.cloned.1.call-update) | async-done | bytes 5242896 | tf_op jit(solution)/shard_map/all_gather | solution.py:11
  596.3 7.2 reshape.219
  603.5 5.6 reduce_sum.77
  609.1 1.8 broadcast_select_fusion.3
  612.8 59.7 %all-gather.29.cloned.1.call-done = f32[10240,256]{0,1:T(8,128)} async-done(((f32[1280,256]{0,1:T(8,128)}), f32[10240,256]{0,1:T(8,128)}) %all-gather.29.cloned.1.call-update) | async-done | bytes 10485776 | tf_op jit(solution)/shard_map/all_gather | solution.py:11
  672.6 8.3 %copy.59 = f32[32,8,8,1280]{3,2,1,0:T(8,128)S(1)} copy(f32[32,8,8,1280]{3,1,2,0:T(8,128)} %bitcast.118) | data formatting | bytes 20971520
  680.9 3.6 bitcast_reduce_fusion.1
  684.4 2.8 copy.47
  687.2 50.4 %all-gather.31.cloned.1.call-done = f32[10240,256]{0,1:T(8,128)} async-done(((f32[1280,256]{0,1:T(8,128)}), f32[10240,256]{0,1:T(8,128)}) %all-gather.31.cloned.1.call-update) | async-done | bytes 10485776 | tf_op jit(solution)/shard_map/all_gather | solution.py:11
  737.6 8.5 %copy.60 = f32[32,8,8,1280]{3,2,1,0:T(8,128)S(1)} copy(f32[32,8,8,1280]{3,1,2,0:T(8,128)} %bitcast.119) | data formatting | bytes 20971520
  746.1 3.5 bitcast_reduce_fusion
  749.6 2.9 copy.48
  755.6 15.0 %convolution_subtract_fusion = f32[1280,2560]{0,1:T(8,128)S(1)} fusion(f32[1280,2560]{0,1:T(8,128)} %copy-done, f32[2560,256]{1,0:T(8,128)S(1)} %bitcast_multiply_fusion, f32[1280,256]{0,1:T(8,128)S(1)} %copy-done.2, f32[1280]{0:T(1024)S(1)} %fusion.54), kind=kOutput, calls=%fused_computation.4 | convolution fusion | flops 10069934080 | bytes 30151680 | tf_op jit(solution)/shard_map/dot_general | solution.py:56
  771.9 5.9 or_select_fusion
  777.8 13.9 %copy.51 = f32[1280,2560]{1,0:T(8,128)} copy(f32[1280,2560]{0,1:T(8,128)} %or_select_fusion) | data formatting | bytes 26214400 | tf_op jit(solution)/shard_map/jit(_where)/select_n | solution.py:64
  (90 shorter events, 26.6 us)
Async XLA Ops:
  6.5 46.6 %all-gather.17.cloned.1.call-start = ((), (), s32[]{:S(2)}) async-start(), calls=%async_computation | async-start | bytes 2359296 | tf_op jit(solution)/shard_map/all_gather | solution.py:11
  22.2 197.4 %all-gather.19.cloned.1.call-start = ((), (), s32[]{:S(2)}) async-start(), calls=%async_computation.1 | async-start | bytes 6553600 | tf_op jit(solution)/shard_map/all_gather | solution.py:11
  121.4 174.3 %all-gather.21.cloned.1.call-start = ((), (), s32[]{:S(2)}) async-start(), calls=%async_computation.2 | async-start | bytes 11796480 | tf_op jit(solution)/shard_map/all_gather | solution.py:11
  234.1 126.5 %all-gather.23.cloned.1.call-start = ((), (), s32[]{:S(2)}) async-start(), calls=%async_computation.3 | async-start | bytes 11796480 | tf_op jit(solution)/shard_map/all_gather | solution.py:11
  234.6 192.3 %all-gather.25.cloned.1.call-start = ((), (), s32[]{:S(2)}) async-start(), calls=%async_computation.4 | async-start | bytes 2359296 | tf_op jit(solution)/shard_map/all_gather | solution.py:11
  372.8 2.9 copy-start.3
  392.9 5.0 copy-start
  398.6 197.7 %all-gather.27.cloned.1.call-start = ((), (), s32[]{:S(2)}) async-start(), calls=%async_computation.5 | async-start | bytes 6553600 | tf_op jit(solution)/shard_map/all_gather | solution.py:11
  498.1 174.4 %all-gather.29.cloned.1.call-start = ((), (), s32[]{:S(2)}) async-start(), calls=%async_computation.6 | async-start | bytes 11796480 | tf_op jit(solution)/shard_map/all_gather | solution.py:11
  609.1 1.9 copy-start.1
  611.0 126.6 %all-gather.31.cloned.1.call-start = ((), (), s32[]{:S(2)}) async-start(), calls=%async_computation.7 | async-start | bytes 11796480 | tf_op jit(solution)/shard_map/all_gather | solution.py:11
  749.6 2.9 copy-start.4
  754.3 1.3 copy-start.2
Sparse Core Ops, SparseCore 0:
  22.3 30.8 all-gather.16
  121.5 98.0 all-gather.18
  234.2 61.4 all-gather.20
  297.4 63.1 all-gather.22
  398.7 28.0 all-gather.24
  498.3 98.0 all-gather.26
  611.1 61.4 all-gather.28
  674.5 63.1 all-gather.30
